TPU v7x, 32 devices: a whole 2x2x4 slice. The times are simulated.
32 devices in a mesh: groups: 2 (over x), seq: 16 (over z, y, core).
Axes of the slice: x: 2, y: 2, z: 4, core: 2. Of those that a mesh axis runs over, the one named last changes fastest.
Arguments:
- query_acts: bfloat16 [4096, 2048], P(('groups', 'seq')), parts along dimension 0, may hold values from -6 to 6
- key_acts: bfloat16 [4096, 2048], P(('groups', 'seq')), parts along dimension 0, may hold values from -6 to 6
- value_acts: bfloat16 [4096, 2048], P(('groups', 'seq')), parts along dimension 0, may hold values from -6 to 6
- beta_logit: float32 [16, 4096], P(None, ('groups', 'seq')), parts along dimension 1, may hold values from -9.3 to 3
- output_grad: bfloat16 [2048, 4096], P('seq', 'groups'), parts along dimension 1, may hold values from -6 to 6
- doc_lengths: int32 [8], P('groups'), parts along dimension 0, may hold values from 1 to 1024, 2048 in all
Outputs:
- query_grad: bfloat16 [2048, 4096], P('seq', 'groups'), parts along dimension 1
- key_grad: bfloat16 [4096, 2048], P(('groups', 'seq')), parts along dimension 0
- value_grad: bfloat16 [4096, 2048], P(('groups', 'seq')), parts along dimension 0
- beta_grad: float32 [16, 4096], P(None, ('groups', 'seq')), parts along dimension 1
There are 2 independent parts, one for each index of `groups`. A program takes and returns all parts, laid end to end along the dimension named above; each array names one. Nothing has to cross between parts.
Inputs may be any that keep to these rules, and one draw needn't show every extreme that they name: `doc_lengths`: the 4 lengths sum to 2048, and the longest has exactly 1024 tokens.
All inputs are finite; a program needn't handle non-finite values.
Results may differ from a plain program's by a relative error of at most 0.001.
Values may be sent and summed in bfloat16 or wider, within the bound.
A program may use at most 192 MiB of HBM per device.

v0:
```python
import jax
import jax.numpy as jnp
from jax import lax
from jax.sharding import PartitionSpec as P

BLOCK = 64


HIGHEST = lax.Precision.HIGHEST


def from_partner(block, axis, bit):
    count = lax.axis_size(axis)
    route = []
    for low in range(count):
        high = low | 1 << bit
        if high != low and high < count:
            route += [(low, high), (high, low)]
    return lax.ppermute(block, axis, route)


def normalize(values):
    return values * lax.rsqrt(jnp.sum(values * values, axis=-1, keepdims=True) + 1e-06)


def count_ends(positions, doc_ends):
    return jnp.sum((positions[:, None] >= doc_ends[None, :]).astype(jnp.int32), axis=1)


def matmul(left, right):
    return jnp.einsum("hij,hjk->hik", left, right, precision=HIGHEST)


def times_transposed(left, right):
    return jnp.einsum("hij,hkj->hik", left, right, precision=HIGHEST)


def block_pass(state_in, queries, keys_norm, values, intensity, doc_ids, prev_docs):
    head_count, length, head_depth = keys_norm.shape
    value_width = values.shape[2]
    blocks = prev_docs.shape[0]
    block_size = length // blocks
    query_blocks = queries.reshape(head_count, blocks, block_size, head_depth)
    key_blocks = keys_norm.reshape(head_count, blocks, block_size, head_depth)
    value_blocks = values.reshape(head_count, blocks, block_size, value_width)
    strength_blocks = intensity.reshape(head_count, blocks, block_size)
    block_ids = doc_ids.reshape(blocks, block_size)
    same_doc = (block_ids[:, :, None] == block_ids[:, None, :]).astype(jnp.float32)
    carried = (block_ids == prev_docs[:, None]).astype(jnp.float32)
    ones_table = jnp.ones((block_size, block_size), jnp.float32)
    strict_lower = jnp.tril(ones_table, -1)
    causal = jnp.tril(ones_table, 0)
    identity = jnp.eye(block_size, dtype=jnp.float32)
    key_gram = jnp.einsum("hncd,hned->hnce", key_blocks, key_blocks, precision=HIGHEST)
    system = identity + strength_blocks[..., :, None] * key_gram * same_doc[None] * strict_lower
    diagonal = identity * strength_blocks[..., :, None]
    solved = lax.linalg.triangular_solve(system, diagonal, left_side=True, lower=True)
    scores = (
        jnp.einsum("hncd,hned->hnce", query_blocks, key_blocks, precision=HIGHEST)
        * (same_doc * causal)[None]
    )
    last_doc = same_doc[:, -1, :]
    keep_state = carried[:, -1]

    def advance(carried_state, inputs):
        solved_b, scores_b, query_b, key_b, value_b, carried_b, last_b, keep_b = inputs
        projected = jnp.einsum("hcd,hvd->hcv", key_b, carried_state, precision=HIGHEST)
        deltas = jnp.einsum(
            "hts,hsv->htv",
            solved_b,
            value_b - carried_b[None, :, None] * projected,
            precision=HIGHEST,
        )
        outputs = carried_b[None, :, None] * jnp.einsum(
            "hcd,hvd->hcv", query_b, carried_state, precision=HIGHEST
        )
        outputs = outputs + jnp.einsum("hts,hsv->htv", scores_b, deltas, precision=HIGHEST)
        new_state = keep_b * carried_state + jnp.einsum(
            "hsv,hsd->hvd", deltas * last_b[None, :, None], key_b, precision=HIGHEST
        )
        return (new_state, outputs)

    inputs = (
        jnp.moveaxis(solved, 1, 0),
        jnp.moveaxis(scores, 1, 0),
        jnp.moveaxis(query_blocks, 1, 0),
        jnp.moveaxis(key_blocks, 1, 0),
        jnp.moveaxis(value_blocks, 1, 0),
        carried,
        last_doc,
        keep_state,
    )
    final_state, block_outs = lax.scan(advance, state_in, inputs)
    block_outs = jnp.moveaxis(block_outs, 0, 1).reshape(head_count, length, value_width)
    return (block_outs, final_state)


def butterfly(transfer, offset, adjoint_seed, identity, zero_state, shard_index, devices):
    totals = (transfer, offset, adjoint_seed)
    prefix = (identity, zero_state)
    suffix = (identity, zero_state)
    for bit_level in range(devices.bit_length() - 1):
        partner = from_partner(totals, "seq", bit_level)
        is_upper = shard_index // 2**bit_level % 2

        def from_lower(operand):
            new_prefix = (matmul(partner[0], prefix[0]), matmul(partner[1], prefix[0]) + prefix[1])
            new_totals = (
                matmul(partner[0], totals[0]),
                matmul(partner[1], totals[0]) + totals[1],
                times_transposed(totals[2], partner[0]) + partner[2],
            )
            return (new_prefix, suffix, new_totals)

        def from_upper(operand):
            new_suffix = (
                matmul(suffix[0], partner[0]),
                times_transposed(partner[2], suffix[0]) + suffix[1],
            )
            new_totals = (
                matmul(totals[0], partner[0]),
                matmul(totals[1], partner[0]) + partner[1],
                times_transposed(partner[2], totals[0]) + totals[2],
            )
            return (prefix, new_suffix, new_totals)

        prefix, suffix, totals = lax.cond(is_upper == 1, from_lower, from_upper, 0)
    return (prefix[1], suffix[1])


def shards(query_acts, key_acts, value_acts, beta_logit, output_grad, doc_lengths):
    devices = lax.axis_size("seq")
    shard_index = lax.axis_index("seq")
    length = query_acts.shape[0]
    head_count = beta_logit.shape[0]
    feature_width = query_acts.shape[1]
    head_depth = feature_width // head_count
    blocks = length // BLOCK
    gathered = lax.all_to_all(output_grad, "seq", split_axis=1, concat_axis=0, tiled=True)
    cotangent = (
        gathered.astype(jnp.float32).reshape(head_count, head_depth, length).transpose(0, 2, 1)
    )
    doc_ends = jnp.cumsum(doc_lengths)
    first_token = shard_index * length
    positions = first_token + jnp.arange(length, dtype=jnp.int32)
    doc_ids = count_ends(positions, doc_ends)
    starts = first_token + jnp.arange(blocks, dtype=jnp.int32) * BLOCK - 1
    prev_docs = jnp.where(starts >= 0, count_ends(starts, doc_ends), -1)

    def split_heads(values):
        return values.reshape(length, head_count, head_depth).transpose(1, 0, 2)

    query_f = query_acts.astype(jnp.float32)
    key_f = key_acts.astype(jnp.float32)
    value_f = value_acts.astype(jnp.float32)
    query_norm = normalize(split_heads(query_f))
    key_norm = normalize(split_heads(key_f))
    value_heads = split_heads(value_f)
    intensity = jax.nn.sigmoid(beta_logit)
    identity = jnp.broadcast_to(
        jnp.eye(head_depth, dtype=jnp.float32), (head_count, head_depth, head_depth)
    )
    zero_state = jnp.zeros((head_count, head_depth, head_depth), jnp.float32)
    lifted_state = jnp.concatenate([identity, zero_state], axis=1)
    lifted_values = jnp.concatenate([jnp.zeros_like(value_heads), value_heads], axis=2)
    lifted_out, lifted_end = block_pass(
        lifted_state, query_norm, key_norm, lifted_values, intensity, doc_ids, prev_docs
    )
    transfer = lifted_end[:, :head_depth]
    offset = lifted_end[:, head_depth:]
    response = lifted_out[..., :head_depth]
    adjoint_seed = jnp.einsum("htv,htd->hvd", cotangent, response, precision=HIGHEST)
    state_in, grad_out = butterfly(
        transfer, offset, adjoint_seed, identity, zero_state, shard_index, devices
    )

    def forward(query_in, key_in, value_in, logit_in):
        return block_pass(
            state_in,
            normalize(split_heads(query_in)),
            normalize(split_heads(key_in)),
            split_heads(value_in),
            jax.nn.sigmoid(logit_in),
            doc_ids,
            prev_docs,
        )

    pullback = jax.vjp(forward, query_f, key_f, value_f, beta_logit)[1]
    grads = pullback((cotangent, grad_out))
    query_local = grads[0].T.astype(jnp.bfloat16)
    query_grad = lax.all_to_all(query_local, "seq", split_axis=0, concat_axis=1, tiled=True)
    return (query_grad, grads[1].astype(jnp.bfloat16), grads[2].astype(jnp.bfloat16), grads[3])


def solution(mesh):
    placed = (
        P(("groups", "seq"), None),
        P(("groups", "seq"), None),
        P(("groups", "seq"), None),
        P(None, ("groups", "seq")),
        P("seq", "groups"),
        P("groups"),
    )
    return jax.shard_map(
        shards,
        mesh=mesh,
        in_specs=placed,
        out_specs=(
            P("seq", "groups"),
            P(("groups", "seq"), None),
            P(("groups", "seq"), None),
            P(None, ("groups", "seq")),
        ),
        check_vma=False,
    )
```

profile of v0, /device:TPU:0, one launch (start us, length us, event | category | flops | bytes accessed | tf_op | source)
XLA Modules:
  0.0 616.7 jit_solution(18337755044069466981)
XLA Ops:
  3.0 7.4 %all-to-all-start = ((bf16[128,16,128]{2,0,1:T(8,128)(2,1)}), bf16[128,16,128]{2,0,1:T(8,128)(2,1)}, u32[]{:S(2)}, u32[]{:S(2)}) async-start(bf16[128,16,128]{2,0,1:T(8,128)(2,1)} %copy.174), calls=%async_computation | async-start | bytes 1048576 | tf_op jit(solution)/shard_map/all_to_all | solution.py:139
  16.0 158.0 %custom-call.7 = f32[16,2,1,64,64]{3,4,2,1,0:T(8,128)S(1)} custom-call(f32[16,2,1,64,64]{4,3,2,1,0:T(8,128)} %select_bitcast_fusion), custom_call_target="InvertDiagBlocksLowerTriangular" | custom-call | tf_op jit(solution)/shard_map/triangular_solve/custom-call.1 | solution.py:57
  193.5 30.6 %while.61 = (s32[]{:T(128)}, f32[16,256,128]{2,1,0:T(8,128)S(1)}, f32[2,16,64,256]{3,2,0,1:T(8,128)}, f32[2]{0:T(128)S(1)}, f32[2,16,64,64]{3,2,1,0:T(8,128)}, /...) while((s32[]{:T(128)}, f32[16,256,128]{2,1,0:T(8,128)S(1)}, ...), condition=%wide.region_6.8_spmd, body=%wide.region_5.7_spmd.sunk | while | flops 1612972032 | bytes 49812008 | solution.py:93
  201.4 5.1 multiply_add_fusion.2
  216.6 5.1 multiply_add_fusion.2
  232.4 18.4 %conditional.4 = (f32[16,128,128]{2,1,0:T(8,128)}, f32[16,128,128]{2,1,0:T(8,128)S(1)}, f32[16,128,128]{2,1,0:T(8,128)}, f32[16,128,128]{2,1,0:T(8,128)S(1)}, f3...) conditional(s32[]{:T(128)} %convert_element_type.105, ...), branch_computations={%region_7.9_spmd, %region_8.10_spmd} | conditional | flops 2013265920 | bytes 41943228 | solution.py:127
  246.4 4.1 fusion.137
  262.6 9.5 %collective-permute-done.3 = f32[16,128,128]{2,1,0:T(8,128)} collective-permute-done((f32[16,128,128]{2,1,0:T(8,128)}, f32[16,128,128]{2,1,0:T(8,128)}, u32[]{:S(2)}, u32[]{:S(2)}) %collective-permute-start.3) | collective-permute-done | bytes 1048608 | tf_op jit(solution)/shard_map/ppermute | solution.py:19
  272.1 22.5 %collective-permute-done.4 = f32[16,128,128]{2,1,0:T(8,128)} collective-permute-done((f32[16,128,128]{2,1,0:T(8,128)}, f32[16,128,128]{2,1,0:T(8,128)}, u32[]{:S(2)}, u32[]{:S(2)}) %collective-permute-start.4) | collective-permute-done | bytes 1048608 | tf_op jit(solution)/shard_map/ppermute | solution.py:19
  294.5 22.5 %collective-permute-done.5 = f32[16,128,128]{2,1,0:T(8,128)} collective-permute-done((f32[16,128,128]{2,1,0:T(8,128)}, f32[16,128,128]{2,1,0:T(8,128)}, u32[]{:S(2)}, u32[]{:S(2)}) %collective-permute-start.5) | collective-permute-done | bytes 1048608 | tf_op jit(solution)/shard_map/ppermute | solution.py:19
  317.0 19.0 %conditional.5 = (f32[16,128,128]{2,1,0:T(8,128)}, f32[16,128,128]{2,1,0:T(8,128)S(1)}, f32[16,128,128]{2,1,0:T(8,128)}, f32[16,128,128]{2,1,0:T(8,128)S(1)}, f3...) conditional(s32[]{:T(128)} %convert_element_type.104, ...), branch_computations={%region_9.11_spmd, %region_10.12_spmd} | conditional | flops 2013528064 | bytes 23068744 | solution.py:127
  331.9 3.8 fusion.146
  344.9 13.4 %collective-permute-done.6 = f32[16,128,128]{2,1,0:T(8,128)} collective-permute-done((f32[16,128,128]{2,1,0:T(8,128)}, f32[16,128,128]{2,1,0:T(8,128)}, u32[]{:S(2)}, u32[]{:S(2)}) %collective-permute-start.6) | collective-permute-done | bytes 1048608 | tf_op jit(solution)/shard_map/ppermute | solution.py:19
  358.3 22.5 %collective-permute-done.7 = f32[16,128,128]{2,1,0:T(8,128)} collective-permute-done((f32[16,128,128]{2,1,0:T(8,128)}, f32[16,128,128]{2,1,0:T(8,128)}, u32[]{:S(2)}, u32[]{:S(2)}) %collective-permute-start.7) | collective-permute-done | bytes 1048608 | tf_op jit(solution)/shard_map/ppermute | solution.py:19
  380.8 22.5 %collective-permute-done.8 = f32[16,128,128]{2,1,0:T(8,128)} collective-permute-done((f32[16,128,128]{2,1,0:T(8,128)}, f32[16,128,128]{2,1,0:T(8,128)}, u32[]{:S(2)}, u32[]{:S(2)}) %collective-permute-start.8) | collective-permute-done | bytes 1048608 | tf_op jit(solution)/shard_map/ppermute | solution.py:19
  403.3 15.5 %conditional.6 = (f32[16,128,128]{2,1,0:T(8,128)}, f32[16,128,128]{2,1,0:T(8,128)S(1)}, f32[16,128,128]{2,1,0:T(8,128)}, f32[16,128,128]{2,1,0:T(8,128)S(1)}, f3...) conditional(s32[]{:T(128)} %convert_element_type.103, ...), branch_computations={%region_11.13_spmd, %region_12.14_spmd} | conditional | flops 1610874880 | bytes 19923008 | solution.py:127
  414.7 3.8 fusion.153
  432.4 58.2 %collective-permute-done.9 = f32[16,128,128]{2,1,0:T(8,128)} collective-permute-done((f32[16,128,128]{2,1,0:T(8,128)}, f32[16,128,128]{2,1,0:T(8,128)}, u32[]{:S(2)}, u32[]{:S(2)}) %collective-permute-start.9) | collective-permute-done | bytes 1048608 | tf_op jit(solution)/shard_map/ppermute | solution.py:19
  490.6 22.5 %collective-permute-done.10 = f32[16,128,128]{2,1,0:T(8,128)} collective-permute-done((f32[16,128,128]{2,1,0:T(8,128)}, f32[16,128,128]{2,1,0:T(8,128)}, u32[]{:S(2)}, u32[]{:S(2)}) %collective-permute-start.10) | collective-permute-done | bytes 1048608 | tf_op jit(solution)/shard_map/ppermute | solution.py:19
  513.1 4.0 conditional.7
  513.1 4.0 convolution_add_fusion.5
  517.1 15.3 %while.62 = (s32[]{:T(128)}, f32[16,128,128]{2,1,0:T(8,128)S(1)}, f32[2,16,128,128]{3,2,1,0:T(8,128)}, f32[2,1,64,1]{2,3,1,0:T(1,128)S(1)}, f32[2,16,64,128]{3,2...) while((s32[]{:T(128)}, f32[16,128,128]{2,1,0:T(8,128)S(1)}, ...), condition=%wide.region_16.18_spmd, body=%wide.region_15.17_spmd.sunk | while | flops 504365056 | bytes 42474388 | solution.py:93
  537.0 34.0 %while.63 = (s32[]{:T(128)}, f32[16,128,128]{2,1,0:T(8,128)S(1)}, f32[2,16,64,64]{3,2,1,0:T(8,128)}, f32[2,16,64,64]{3,2,1,0:T(8,128)}, f32[2,16,64,128]{3,2,0,1...) while((s32[]{:T(128)}, f32[16,128,128]{2,1,0:T(8,128)S(1)}, ...), condition=%wide.region_18.20_spmd, body=%wide.region_17.19_spmd.sunk | while | flops 1612578816 | bytes 77082800 | solution.py:93
  576.3 17.3 %all-to-all-start.1 = ((bf16[16,128,128]{2,1,0:T(8,128)(2,1)}), bf16[16,128,128]{2,1,0:T(8,128)(2,1)}, u32[]{:S(2)}, u32[]{:S(2)}) async-start(bf16[16,128,128]{2,1,0:T(8,128)(2,1)} %fusion.121), calls=%async_computation.1 | async-start | bytes 1048576 | tf_op jit(solution)/shard_map/all_to_all | solution.py:191
  (343 shorter events, 209.9 us)
Async XLA Ops:
  0.6 9.9 %copy-start.59 = (s32[4]{0:T(128)S(1)}, s32[4]{0:T(128)}, u32[]{:S(2)}) copy-start(s32[4]{0:T(128)} %param.29) | copy-start | bytes 52
  0.6 10.6 %copy-start.56 = (bf16[128,2048]{1,0:T(8,128)(2,1)S(1)}, bf16[128,2048]{1,0:T(8,128)(2,1)}, u32[]{:S(2)}) copy-start(bf16[128,2048]{1,0:T(8,128)(2,1)} %param.25) | copy-start | bytes 1572868
  3.0 223.2 %all-to-all-start = ((bf16[128,16,128]{2,0,1:T(8,128)(2,1)}), bf16[128,16,128]{2,0,1:T(8,128)(2,1)}, u32[]{:S(2)}, u32[]{:S(2)}) async-start(bf16[128,16,128]{2,0,1:T(8,128)(2,1)} %copy.174), calls=%async_computation | async-start | bytes 1048576 | tf_op jit(solution)/shard_map/all_to_all | solution.py:139
  12.3 169.6 %copy-start.1 = (f32[16,128,128]{2,1,0:T(8,128)}, f32[16,128,128]{2,1,0:T(8,128)S(1)}, u32[]{:S(2)}) copy-start(f32[16,128,128]{2,1,0:T(8,128)S(1)} %copy.155) | copy-start | bytes 3145732
  201.4 5.1 copy-start.7
  201.4 5.1 copy-start.54
  216.6 5.1 copy-start.7
  216.6 5.1 copy-start.54
  225.7 4.2 collective-permute-start
  226.0 4.2 collective-permute-start.2
  229.5 2.9 collective-permute-start.1
  250.8 21.3 %collective-permute-start.3 = (f32[16,128,128]{2,1,0:T(8,128)}, f32[16,128,128]{2,1,0:T(8,128)}, u32[]{:S(2)}, u32[]{:S(2)}) collective-permute-start(f32[16,128,128]{2,1,0:T(8,128)} %get-tuple-element.1142), channel_id=1, source_target_pairs={{0,2},{2,0},{1,3},{3,1},{4,6},{6,4},{5,7},{7,5},{8,10},{10,8},{9,1... | collective-permute-start | bytes 3145736 | tf_op jit(solution)/shard_map/ppermute | solution.py:19
  257.9 36.6 %collective-permute-start.4 = (f32[16,128,128]{2,1,0:T(8,128)}, f32[16,128,128]{2,1,0:T(8,128)}, u32[]{:S(2)}, u32[]{:S(2)}) collective-permute-start(f32[16,128,128]{2,1,0:T(8,128)} %add.207), channel_id=1, source_target_pairs={{0,2},{2,0},{1,3},{3,1},{4,6},{6,4},{5,7},{7,5},{8,10},{10,8},{9,1... | collective-permute-start | bytes 3145736 | tf_op jit(solution)/shard_map/ppermute | solution.py:19
  260.7 56.3 %collective-permute-start.5 = (f32[16,128,128]{2,1,0:T(8,128)}, f32[16,128,128]{2,1,0:T(8,128)}, u32[]{:S(2)}, u32[]{:S(2)}) collective-permute-start(f32[16,128,128]{2,1,0:T(8,128)} %add.208), channel_id=1, source_target_pairs={{0,2},{2,0},{1,3},{3,1},{4,6},{6,4},{5,7},{7,5},{8,10},{10,8},{9,1... | collective-permute-start | bytes 3145736 | tf_op jit(solution)/shard_map/ppermute | solution.py:19
  336.0 22.3 %collective-permute-start.6 = (f32[16,128,128]{2,1,0:T(8,128)}, f32[16,128,128]{2,1,0:T(8,128)}, u32[]{:S(2)}, u32[]{:S(2)}) collective-permute-start(f32[16,128,128]{2,1,0:T(8,128)} %get-tuple-element.853), channel_id=1, source_target_pairs={{0,4},{4,0},{1,5},{5,1},{2,6},{6,2},{3,7},{7,3},{8,12},{12,8},{9,1... | collective-permute-start | bytes 3145736 | tf_op jit(solution)/shard_map/ppermute | solution.py:19
  340.5 40.3 %collective-permute-start.7 = (f32[16,128,128]{2,1,0:T(8,128)}, f32[16,128,128]{2,1,0:T(8,128)}, u32[]{:S(2)}, u32[]{:S(2)}) collective-permute-start(f32[16,128,128]{2,1,0:T(8,128)} %add.209), channel_id=1, source_target_pairs={{0,4},{4,0},{1,5},{5,1},{2,6},{6,2},{3,7},{7,3},{8,12},{12,8},{9,1... | collective-permute-start | bytes 3145736 | tf_op jit(solution)/shard_map/ppermute | solution.py:19
  342.9 60.4 %collective-permute-start.8 = (f32[16,128,128]{2,1,0:T(8,128)}, f32[16,128,128]{2,1,0:T(8,128)}, u32[]{:S(2)}, u32[]{:S(2)}) collective-permute-start(f32[16,128,128]{2,1,0:T(8,128)} %add.210), channel_id=1, source_target_pairs={{0,4},{4,0},{1,5},{5,1},{2,6},{6,2},{3,7},{7,3},{8,12},{12,8},{9,1... | collective-permute-start | bytes 3145736 | tf_op jit(solution)/shard_map/ppermute | solution.py:19
  421.1 69.5 %collective-permute-start.9 = (f32[16,128,128]{2,1,0:T(8,128)}, f32[16,128,128]{2,1,0:T(8,128)}, u32[]{:S(2)}, u32[]{:S(2)}) collective-permute-start(f32[16,128,128]{2,1,0:T(8,128)} %add.211), channel_id=1, source_target_pairs={{0,8},{8,0},{1,9},{9,1},{2,10},{10,2},{3,11},{11,3},{4,12},{12,4},... | collective-permute-start | bytes 3145736 | tf_op jit(solution)/shard_map/ppermute | solution.py:19
  426.7 86.3 %collective-permute-start.10 = (f32[16,128,128]{2,1,0:T(8,128)}, f32[16,128,128]{2,1,0:T(8,128)}, u32[]{:S(2)}, u32[]{:S(2)}) collective-permute-start(f32[16,128,128]{2,1,0:T(8,128)} %add.212), channel_id=1, source_target_pairs={{0,8},{8,0},{1,9},{9,1},{2,10},{10,2},{3,11},{11,3},{4,12},{12,4},... | collective-permute-start | bytes 3145736 | tf_op jit(solution)/shard_map/ppermute | solution.py:19
  532.4 4.6 copy-start
  545.7 5.0 copy-start.47
  562.6 5.0 copy-start.47
  575.1 18.5 %copy-start.20 = (f32[16,128,128]{2,1,0:T(8,128)S(1)}, f32[16,128,128]{2,1,0:T(8,128)}, u32[]{:S(2)}) copy-start(f32[16,128,128]{2,1,0:T(8,128)} %copy-done.18) | copy-start | bytes 3145732
  576.3 37.6 %all-to-all-start.1 = ((bf16[16,128,128]{2,1,0:T(8,128)(2,1)}), bf16[16,128,128]{2,1,0:T(8,128)(2,1)}, u32[]{:S(2)}, u32[]{:S(2)}) async-start(bf16[16,128,128]{2,1,0:T(8,128)(2,1)} %fusion.121), calls=%async_computation.1 | async-start | bytes 1048576 | tf_op jit(solution)/shard_map/all_to_all | solution.py:191
  (74 other events, 183.4 us)
where the time goes:
time: 626 us; the launch traced here: 617 us
  waiting for transfers between devices  196 us (31%)
  other arithmetic  183 us (29%)
  matrix products  147 us (23%)
  local copies, waits for them, and re-layouts  50 us (8%)
  starting transfers between devices  36.9 us (6%)
    ppermute x11, waiting for transfers between devices, from_partner(): return lax.ppermute(block, axis, route)  196 us
    another operation x3, other arithmetic, block_pass(): lax.linalg.triangular_solve(system, diagonal, left_side=True, lower=True)  159 us
    dot_general x8, matrix products, matmul(): return jnp.einsum('hij,hjk->hik', left, right, precision=HIGHEST)  26.5 us
    dot_general x7, matrix products, times_transposed(): return jnp.einsum('hij,hkj->hik', left, right, precision=HIGHEST)  26.4 us
    dot_general x8, matrix products, advance(): jnp.einsum('hsv,hsd->hvd', deltas * last_b[None, :, None], key_b, precisi...  24.5 us
    all_to_all x1, starting transfers between devices, shards(): lax.all_to_all(query_local, 'seq', split_axis=0, concat_axis=1, tiled=True)  17.3 us
    dot_general x8, matrix products, advance(): jnp.einsum('hcd,hvd->hcv', key_b, carried_state, precision=HIGHEST)  15.1 us
    dot_general x6, matrix products, advance(): jnp.einsum('hcd,hvd->hcv', query_b, carried_state, precision=HIGHEST)  14.3 us
  transfers between devices with their start and end apart: 13, of which 10 were waited for; matrix products, arithmetic and copies ran while one was open for 41% of the time, Pallas kernels for 0%

commit v1 on v0

--- a/solution.py
+++ b/solution.py
@@ -1,9 +1,251 @@
+import functools
 import jax
 import jax.numpy as jnp
 from jax import lax
+from jax.experimental import pallas as pl
+from jax.experimental.pallas import tpu as pltpu
 from jax.sharding import PartitionSpec as P
 
 BLOCK = 64
+CHUNK = 128
+GROUP = 4
+F32 = jnp.float32
+BF16 = jnp.bfloat16
+
+
+def dot(left, right, dims):
+    return lax.dot_general(left, right, ((dims[:1], dims[1:]), ((), ())), preferred_element_type=F32)
+
+
+def split(values):
+    high = values.astype(BF16)
+    return high, (values - high.astype(F32)).astype(BF16)
+
+
+def dot2l(left, exact, dims=(1, 0)):
+    high, low = left
+    return dot(high, exact, dims) + dot(low, exact, dims)
+
+
+def dot2r(exact, right, dims=(1, 0)):
+    high, low = right
+    return dot(exact, high, dims) + dot(exact, low, dims)
+
+
+def dot3(left, right, dims=(1, 0)):
+    return dot(left[0], right[0], dims) + (dot(left[1], right[0], dims) + dot(left[0], right[1], dims))
+
+
+def across(column):
+    return jnp.broadcast_to(column, (CHUNK, CHUNK)).T
+
+
+def inverse_norm(values):
+    wide = values.astype(F32)
+    return lax.rsqrt(jnp.sum(wide * wide, axis=1, keepdims=True) + 1e-06)
+
+
+def doc_of(positions, ends):
+    total = jnp.zeros(jnp.shape(positions), jnp.int32)
+    for end in ends:
+        total = total + (positions >= end).astype(jnp.int32)
+    return total
+
+
+def chunk_masks(index, ends):
+    first = index * CHUNK
+    down = first + lax.broadcasted_iota(jnp.int32, (CHUNK, CHUNK), 0)
+    over = first + lax.broadcasted_iota(jnp.int32, (CHUNK, CHUNK), 1)
+    doc_down = doc_of(down, ends)
+    doc_over = doc_of(over, ends)
+    before = jnp.where(first > 0, doc_of(first - 1, ends), -1)
+    last = doc_of(first + CHUNK - 1, ends)
+    same = doc_down == doc_over
+    causal = jnp.where(same & (down >= over), 1.0, 0.0)
+    strict = jnp.where(same & (down > over), 1.0, 0.0)
+    carried = jnp.where(doc_down == before, 1.0, 0.0)
+    closing = jnp.where(doc_down == last, 1.0, 0.0)
+    keep = jnp.where(before == last, 1.0, 0.0)
+    return causal, strict, carried, closing, keep
+
+
+def invert(systems):
+    rows = lax.broadcasted_iota(jnp.int32, (CHUNK, CHUNK), 0)
+    cols = lax.broadcasted_iota(jnp.int32, (CHUNK, CHUNK), 1)
+    eye = jnp.where(rows == cols, 1.0, 0.0)
+    size = 1
+    solved = None
+    while size < CHUNK:
+        pair = (rows // (2 * size) == cols // (2 * size)) & (rows // size != cols // size)
+        corners = [jnp.where(pair, system, 0.0) for system in systems]
+        if solved is None:
+            solved = [eye - corner for corner in corners]
+        else:
+            parts = [split(value) for value in solved]
+            inner = [dot3(split(corner), part) for corner, part in zip(corners, parts)]
+            solved = [
+                value - dot3(part, split(middle))
+                for value, part, middle in zip(solved, parts, inner)
+            ]
+        size *= 2
+    return solved
+
+
+def ends_of(lengths_ref):
+    ends = []
+    total = 0
+    for i in range(lengths_ref.shape[0]):
+        total = total + lengths_ref[i]
+        ends.append(total)
+    return ends
+
+
+def prepare(indices, ends, load, store):
+    items = []
+    for index in indices:
+        query, key, value, cotangent, strength = load(index)
+        causal, strict, carried, closing, keep = chunk_masks(index, ends)
+        norm_q, norm_k = inverse_norm(query), inverse_norm(key)
+        key_over = across(norm_k)
+        gram = dot(key, key, (1, 1)) * norm_k * key_over
+        scores = dot(query, key, (1, 1)) * norm_q * key_over * causal
+        strength_down = strength.T
+        items.append(
+            (index, query, key, value, cotangent, carried, closing, keep, norm_q, norm_k,
+             key_over, scores, strength, strength_down * gram * strict)
+        )
+    solved = invert([item[-1] for item in items])
+    for item, inverse in zip(items, solved):
+        (index, query, key, value, cotangent, carried, closing, keep, norm_q, norm_k,
+         key_over, scores, strength, _) = item
+        weighted = inverse * strength
+        local = dot2l(split(weighted), value)
+        response_k = dot2l(split(weighted * key_over * carried.T), key)
+        ending = dot2l(split((weighted * (closing * norm_k)).T), key)
+        offset = dot2r(value, split(ending), (0, 0))
+        step = dot2r(key, split(ending * (carried * norm_k)), (0, 0))
+        scores_parts = split(scores)
+        response = carried * norm_q * query.astype(F32) - dot3(scores_parts, split(response_k))
+        seed = dot2r(cotangent, split(response))
+        early = dot2l(split(scores.T), cotangent, (1, 1))
+        store(index, inverse, scores, local, response_k, offset, step, seed, early)
+
+
+def finish(index, ends, load, stored, state, adjoint):
+    query, key, value, cotangent, strength = load(index)
+    inverse, scores, local, response_k, early = stored
+    causal, strict, carried, closing, keep = chunk_masks(index, ends)
+    norm_q, norm_k = inverse_norm(query), inverse_norm(key)
+    key_f = key.astype(F32) * norm_k
+    query_f = query.astype(F32) * norm_q
+    key_over = across(norm_k)
+    query_over = across(norm_q)
+    strength_down = strength.T
+    state_parts = split(state)
+    adjoint_parts = split(adjoint)
+    turned = cotangent.astype(F32).T.astype(BF16)
+    deltas = local - dot3(split(response_k), state_parts, (1, 1))
+    delta_parts = split(deltas)
+    delta_grad = early + closing * norm_k * dot2r(key, adjoint_parts, (1, 1))
+    right_grad = dot3(split(inverse.T), split(delta_grad))
+    value_grad = strength_down * right_grad
+    logit_grad = (1.0 - strength_down) * jnp.sum(right_grad * deltas, axis=1, keepdims=True)
+    system_grad = -strength_down * strict * dot3(split(right_grad), delta_parts, (1, 1))
+    scores_grad = causal * dot2r(turned, delta_parts, (1, 1))
+    gram_grad = system_grad + system_grad.T
+    query_norm_grad = dot2l(split(scores_grad * key_over), key)
+    query_norm_grad = query_norm_grad + carried * dot2r(turned, state_parts)
+    key_norm_grad = dot2l(split(gram_grad * key_over), key)
+    key_norm_grad = key_norm_grad + dot2l(split(scores_grad.T * query_over), query)
+    key_norm_grad = key_norm_grad + dot3(split(closing * deltas), adjoint_parts)
+    key_norm_grad = key_norm_grad - dot3(split(carried * value_grad), state_parts)
+    query_grad = norm_q * (
+        query_norm_grad - query_f * jnp.sum(query_f * query_norm_grad, axis=1, keepdims=True)
+    )
+    key_grad = norm_k * (
+        key_norm_grad - key_f * jnp.sum(key_f * key_norm_grad, axis=1, keepdims=True)
+    )
+    return query_grad.T.astype(BF16), key_grad.astype(BF16), value_grad.astype(BF16), across(logit_grad)[:1]
+
+
+def head_kernel(
+    lengths_ref, query_ref, key_ref, value_ref, logit_ref, cotangent_ref,
+    query_out, key_out, value_out, logit_out,
+    inverse_ref, scores_ref, local_ref, response_ref, offset_ref, step_ref, seed_ref, early_ref,
+    state_ref, adjoint_ref,
+):
+    chunks = query_ref.shape[0]
+    ends = ends_of(lengths_ref)
+
+    def load(index):
+        logit = jnp.broadcast_to(logit_ref[index], (CHUNK, CHUNK))
+        strength = 1.0 / (1.0 + jnp.exp(-logit))
+        return query_ref[index], key_ref[index], value_ref[index], cotangent_ref[index], strength
+
+    def store(index, inverse, scores, local, response_k, offset, step, seed, early):
+        inverse_ref[index] = inverse
+        scores_ref[index] = scores
+        local_ref[index] = local
+        response_ref[index] = response_k
+        offset_ref[index] = offset
+        step_ref[index] = step
+        seed_ref[index] = seed
+        early_ref[index] = early
+
+    def early_body(turn, carry):
+        prepare([turn * GROUP + i for i in range(GROUP)], ends, load, store)
+        return carry
+
+    lax.fori_loop(0, chunks // GROUP, early_body, 0)
+
+    def keep_of(index):
+        first = index * CHUNK
+        before = jnp.where(first > 0, doc_of(first - 1, ends), -1)
+        return jnp.where(before == doc_of(first + CHUNK - 1, ends), 1.0, 0.0)
+
+    def chain(turn, carry):
+        state, adjoint = carry
+        back = chunks - 1 - turn
+        state_ref[turn] = state
+        adjoint_ref[back] = adjoint
+        moved = dot3(split(state), split(step_ref[turn]))
+        pulled = dot3(split(adjoint), split(step_ref[back]), (1, 1))
+        state = keep_of(turn) * state - moved + offset_ref[turn]
+        adjoint = keep_of(back) * adjoint - pulled + seed_ref[back]
+        return state, adjoint
+
+    zero = jnp.zeros((CHUNK, CHUNK), F32)
+    lax.fori_loop(0, chunks, chain, (zero, zero))
+
+    def late_body(turn, carry):
+        for i in range(2):
+            index = turn * 2 + i
+            stored = (inverse_ref[index], scores_ref[index], local_ref[index],
+                      response_ref[index], early_ref[index])
+            results = finish(index, ends, load, stored, state_ref[index], adjoint_ref[index])
+            query_out[index] = results[0]
+            key_out[index] = results[1]
+            value_out[index] = results[2]
+            logit_out[index] = results[3]
+        return carry
+
+    lax.fori_loop(0, chunks // 2, late_body, 0)
+
+
+def head_pass(query, key, value, logit, cotangent, lengths, interpret=False):
+    chunks = query.shape[0]
+    square = (chunks, CHUNK, CHUNK)
+    whole = pl.BlockSpec(memory_space=pltpu.VMEM)
+    return pl.pallas_call(
+        head_kernel,
+        in_specs=[pl.BlockSpec(memory_space=pltpu.SMEM)] + [whole] * 5,
+        out_specs=[whole] * 4,
+        out_shape=[jax.ShapeDtypeStruct(square, BF16)] * 3
+        + [jax.ShapeDtypeStruct((chunks, 1, CHUNK), F32)],
+        scratch_shapes=[pltpu.VMEM(square, F32)] * 10,
+        compiler_params=pltpu.CompilerParams(vmem_limit_bytes=48 << 20),
+        interpret=interpret,
+    )(lengths, query, key, value, logit, cotangent)
 
 
 HIGHEST = lax.Precision.HIGHEST
@@ -128,7 +370,7 @@
     return (prefix[1], suffix[1])
 
 
-def shards(query_acts, key_acts, value_acts, beta_logit, output_grad, doc_lengths):
+def shards_by_tokens(query_acts, key_acts, value_acts, beta_logit, output_grad, doc_lengths):
     devices = lax.axis_size("seq")
     shard_index = lax.axis_index("seq")
     length = query_acts.shape[0]
@@ -190,6 +432,44 @@
     query_local = grads[0].T.astype(jnp.bfloat16)
     query_grad = lax.all_to_all(query_local, "seq", split_axis=0, concat_axis=1, tiled=True)
     return (query_grad, grads[1].astype(jnp.bfloat16), grads[2].astype(jnp.bfloat16), grads[3])
+
+
+def shards(query_acts, key_acts, value_acts, beta_logit, output_grad, doc_lengths):
+    devices = lax.axis_size("seq")
+    length, width = query_acts.shape
+    head_count = beta_logit.shape[0]
+    window = length * devices
+    chunks = window // CHUNK
+    by_heads = devices == head_count and width == head_count * CHUNK and chunks % GROUP == 0
+    if not by_heads or window % CHUNK:
+        return shards_by_tokens(
+            query_acts, key_acts, value_acts, beta_logit, output_grad, doc_lengths
+        )
+
+    def to_heads(values):
+        moved = lax.all_to_all(values, "seq", split_axis=1, concat_axis=0, tiled=True)
+        return moved.reshape(chunks, CHUNK, CHUNK)
+
+    def to_tokens(values):
+        return lax.all_to_all(
+            values.reshape(window, CHUNK), "seq", split_axis=0, concat_axis=1, tiled=True
+        )
+
+    logit = lax.all_to_all(beta_logit, "seq", split_axis=0, concat_axis=1, tiled=True)
+    cotangent = output_grad.reshape(CHUNK, chunks, CHUNK).transpose(1, 0, 2)
+    grads = head_pass(
+        to_heads(query_acts),
+        to_heads(key_acts),
+        to_heads(value_acts),
+        logit.reshape(chunks, 1, CHUNK),
+        cotangent,
+        doc_lengths,
+    )
+    query_grad = grads[0].transpose(1, 0, 2).reshape(CHUNK, window)
+    logit_grad = lax.all_to_all(
+        grads[3].reshape(1, window), "seq", split_axis=1, concat_axis=0, tiled=True
+    )
+    return query_grad, to_tokens(grads[1]), to_tokens(grads[2]), logit_grad
 
 
 def solution(mesh):

time: 626 us -> 156 us (0.25); the launches traced: 617 us -> 155 us
  other arithmetic: 183 us -> 0 us
  matrix products: 147 us -> 0 us
  waiting for transfers between devices: 196 us -> 56 us
  local copies, waits for them, and re-layouts: 50 us -> 10.7 us
  Pallas kernels: 0 us -> 37.1 us
  blocking collectives: 0 us -> 27.4 us
  starting transfers between devices: 36.9 us -> 23.1 us
    ppermute x11 -> x0, waiting for transfers between devices: 196 us -> none  [from_partner(): return lax.ppermute(block, axis, route)]
    another operation x9 -> x0, other arithmetic: 160 us -> none  [the longest x3 159 us: block_pass(): lax.linalg.triangular_solve(system, diagonal, left_side=True, lower=True)]
    dot_general x59 -> x0, matrix products: 141 us -> none  [the longest x8 26.5 us: matmul(): return jnp.einsum('hij,hjk->hik', left, right, precision=HIGHEST)]
    all_to_all x2 -> x5, waiting for transfers between devices: 0.01 us -> 56 us  [the longest x3 40.1 us: to_heads(): lax.all_to_all(values, 'seq', split_axis=1, concat_axis=0, tiled=True)]
    pallas_call x0 -> x1, Pallas kernels: none -> 37.1 us  [head_pass(): pl.pallas_call(head_kernel, in_specs=[pl.BlockSpec(memory_space=pltpu.SME...]
    all_to_all x0 -> x2, blocking collectives: none -> 27.4 us  [the longest x1 17.1 us: to_tokens(): lax.all_to_all(values.reshape(window, CHUNK), 'seq', split_axis=0, concat...]
    add x8 -> x0, other arithmetic: 14.8 us -> none  [the longest x3 7.4 us: from_upper(): times_transposed(partner[2], totals[0]) + totals[2]]
    ppermute x11 -> x0, starting transfers between devices: 12.2 us -> none  [from_partner(): return lax.ppermute(block, axis, route)]
  transfers between devices with their start and end apart: 13 -> 5, of which waited for: 10 -> 5; matrix products, arithmetic and copies ran while one was open for 41% -> 5% of each run, Pallas kernels for 0% -> 0%
where the time goes in v1:
time: 156 us; the launch traced here: 155 us
  waiting for transfers between devices  56 us (36%)
  Pallas kernels  37.1 us (24%)
  blocking collectives  27.4 us (18%)
  starting transfers between devices  23.1 us (15%)
  local copies, waits for them, and re-layouts  10.7 us (7%)
    all_to_all x3, waiting for transfers between devices, to_heads(): lax.all_to_all(values, 'seq', split_axis=1, concat_axis=0, tiled=True)  40.1 us
    pallas_call x1, Pallas kernels, head_pass(): pl.pallas_call(head_kernel, in_specs=[pl.BlockSpec(memory_space=pltpu.SME...  37.1 us
    all_to_all x1, blocking collectives, to_tokens(): lax.all_to_all(values.reshape(window, CHUNK), 'seq', split_axis=0, concat...  17.1 us
    all_to_all x1, waiting for transfers between devices, to_tokens(): lax.all_to_all(values.reshape(window, CHUNK), 'seq', split_axis=0, concat...  11.8 us
    all_to_all x3, starting transfers between devices, to_heads(): lax.all_to_all(values, 'seq', split_axis=1, concat_axis=0, tiled=True)  11.7 us
    all_to_all x1, blocking collectives, shards(): lax.all_to_all(grads[3].reshape(1, window), 'seq', split_axis=1, concat_a...  10.3 us
    all_to_all x1, starting transfers between devices, shards(): lax.all_to_all(beta_logit, 'seq', split_axis=0, concat_axis=1, tiled=True)  7.4 us
    unnamed x16, local copies, waits for them, and re-layouts  6.45 us
  transfers between devices with their start and end apart: 5, of which 5 were waited for; matrix products, arithmetic and copies ran while one was open for 5% of the time, Pallas kernels for 0%

profile of v1, /device:TPU:0, one launch (start us, length us, event | category | flops | bytes accessed | tf_op | source)
XLA Modules:
  0.0 155.0 jit_solution(12910074664768350556)
XLA Ops:
  0.6 7.4 %all-to-all-start.3 = ((f32[16,1,128]{2,1,0:T(1,128)}), f32[16,1,128]{2,1,0:T(1,128)S(1)}, u32[]{:S(2)}, u32[]{:S(2)}) async-start(f32[16,1,128]{2,1,0:T(1,128)} %bitcast.35), calls=%async_computation.3 | async-start | bytes 16384 | tf_op jit(solution)/shard_map/all_to_all | solution.py:458
  8.0 1.3 copy.24
  9.4 1.0 copy.25
  10.4 4.0 %all-to-all-done.3.logit_ref = f32[16,1,128]{2,1,0:T(1,128)S(1)} async-done(((f32[16,1,128]{2,1,0:T(1,128)}), f32[16,1,128]{2,1,0:T(1,128)S(1)}, u32[]{:S(2)}, u32[]{:S(2)}) %all-to-all-start.3) | async-done | bytes 8224 | tf_op jit(solution)/shard_map/all_to_all | solution.py:458
  14.4 3.6 %all-to-all-start = ((bf16[128,16,128]{2,0,1:T(8,128)(2,1)}), bf16[128,16,128]{2,0,1:T(8,128)(2,1)S(1)}, u32[]{:S(2)}, u32[]{:S(2)}) async-start(bf16[128,16,128]{2,0,1:T(8,128)(2,1)} %copy.25), calls=%async_computation | async-start | bytes 1048576 | tf_op jit(solution)/shard_map/all_to_all | solution.py:450
  18.2 1.0 copy.27
  19.3 13.1 %all-to-all-done = bf16[128,16,128]{2,0,1:T(8,128)(2,1)S(1)} async-done(((bf16[128,16,128]{2,0,1:T(8,128)(2,1)}), bf16[128,16,128]{2,0,1:T(8,128)(2,1)S(1)}, u32[]{:S(2)}, u32[]{:S(2)}) %all-to-all-start) | async-done | bytes 524320 | tf_op jit(solution)/shard_map/all_to_all | solution.py:450
  32.4 4.0 %all-to-all-start.1 = ((bf16[128,16,128]{2,0,1:T(8,128)(2,1)}), bf16[128,16,128]{2,0,1:T(8,128)(2,1)S(1)}, u32[]{:S(2)}, u32[]{:S(2)}) async-start(bf16[128,16,128]{2,0,1:T(8,128)(2,1)} %copy.27), calls=%async_computation.1 | async-start | bytes 1048576 | tf_op jit(solution)/shard_map/all_to_all | solution.py:450
  36.7 1.0 copy.29
  37.7 13.2 %all-to-all-done.1 = bf16[128,16,128]{2,0,1:T(8,128)(2,1)S(1)} async-done(((bf16[128,16,128]{2,0,1:T(8,128)(2,1)}), bf16[128,16,128]{2,0,1:T(8,128)(2,1)S(1)}, u32[]{:S(2)}, u32[]{:S(2)}) %all-to-all-start.1) | async-done | bytes 524320 | tf_op jit(solution)/shard_map/all_to_all | solution.py:450
  50.9 4.1 %all-to-all-start.2 = ((bf16[128,16,128]{2,0,1:T(8,128)(2,1)}), bf16[128,16,128]{2,0,1:T(8,128)(2,1)S(1)}, u32[]{:S(2)}, u32[]{:S(2)}) async-start(bf16[128,16,128]{2,0,1:T(8,128)(2,1)} %copy.29), calls=%async_computation.2 | async-start | bytes 1048576 | tf_op jit(solution)/shard_map/all_to_all | solution.py:450
  55.3 0.3 copy.31
  55.6 13.9 %all-to-all-done.2 = bf16[128,16,128]{2,0,1:T(8,128)(2,1)S(1)} async-done(((bf16[128,16,128]{2,0,1:T(8,128)(2,1)}), bf16[128,16,128]{2,0,1:T(8,128)(2,1)S(1)}, u32[]{:S(2)}, u32[]{:S(2)}) %all-to-all-start.2) | async-done | bytes 524320 | tf_op jit(solution)/shard_map/all_to_all | solution.py:450
  69.4 0.7 copy-done
  70.1 37.1 %shard_map.93 = (bf16[16,128,128]{2,1,0:T(8,128)(2,1)S(1)}, bf16[16,128,128]{2,1,0:T(8,128)(2,1)S(1)}, bf16[16,128,128]{2,1,0:T(8,128)(2,1)}, f32[16,1,128]{2,1,0:T(1,128)S(1)}) custom-call(s32[4]{0:T(128)S(1)} %copy-done, bf16[16,128,128]{2,1,0:T(8,128)(2,1)S(1)} %bitcast.19, bf16[16,128,128]{2,1,0:T(8,128)(2,1)S(1)} %bitcast.20, ...), custom_call_target="tpu_custom_call" | custom-call | tf_op jit(solution)/shard_map/pallas_call | solution.py:239
  107.2 10.3 %all_to_all.109 = f32[1,16,128]{2,0,1:T(1,128)S(1)} all-to-all(f32[1,16,128]{2,0,1:T(1,128)S(1)} %bitcast.24), channel_id=1, replica_groups=mesh['groups'=2,'seq'=16] {'seq'}, dimensions={1} | all-to-all | bytes 16384 | tf_op jit(solution)/shard_map/all_to_all | solution.py:469
  117.5 17.1 %all_to_all.110 = bf16[16,128,128]{2,1,0:T(8,128)(2,1)S(1)} all-to-all(bf16[16,128,128]{2,1,0:T(8,128)(2,1)S(1)} %get-tuple-element.9), channel_id=1, replica_groups=mesh['groups'=2,'seq'=16] {'seq'}, dimensions={0} | all-to-all | bytes 1048576 | tf_op jit(solution)/shard_map/all_to_all | solution.py:454
  134.6 4.0 %all-to-all-start.5 = ((bf16[16,128,128]{2,1,0:T(8,128)(2,1)}), bf16[16,128,128]{2,1,0:T(8,128)(2,1)S(1)}, u32[]{:S(2)}, u32[]{:S(2)}) async-start(bf16[16,128,128]{2,1,0:T(8,128)(2,1)} %get-tuple-element.10), calls=%async_computation.5 | async-start | bytes 1048576 | tf_op jit(solution)/shard_map/all_to_all | solution.py:454
  138.6 0.3 copy.32
  138.9 1.0 copy.36
  140.2 1.0 copy.37
  141.3 11.8 %all-to-all-done.5 = bf16[16,128,128]{2,1,0:T(8,128)(2,1)S(1)} async-done(((bf16[16,128,128]{2,1,0:T(8,128)(2,1)}), bf16[16,128,128]{2,1,0:T(8,128)(2,1)S(1)}, u32[]{:S(2)}, u32[]{:S(2)}) %all-to-all-start.5) | async-done | bytes 524320 | tf_op jit(solution)/shard_map/all_to_all | solution.py:454
  153.4 1.0 copy.38
  154.4 0.6 copy.40
  (12 shorter events, 1.4 us)
Async XLA Ops:
  0.6 13.7 %all-to-all-start.3 = ((f32[16,1,128]{2,1,0:T(1,128)}), f32[16,1,128]{2,1,0:T(1,128)S(1)}, u32[]{:S(2)}, u32[]{:S(2)}) async-start(f32[16,1,128]{2,1,0:T(1,128)} %bitcast.35), calls=%async_computation.3 | async-start | bytes 16384 | tf_op jit(solution)/shard_map/all_to_all | solution.py:458
  10.4 7.6 %copy-start.1 = (bf16[128,2048]{1,0:T(8,128)(2,1)S(1)}, bf16[128,2048]{1,0:T(8,128)(2,1)}, u32[]{:S(2)}) copy-start(bf16[128,2048]{1,0:T(8,128)(2,1)} %param.7) | copy-start | bytes 1572868
  14.4 18.0 %all-to-all-start = ((bf16[128,16,128]{2,0,1:T(8,128)(2,1)}), bf16[128,16,128]{2,0,1:T(8,128)(2,1)S(1)}, u32[]{:S(2)}, u32[]{:S(2)}) async-start(bf16[128,16,128]{2,0,1:T(8,128)(2,1)} %copy.25), calls=%async_computation | async-start | bytes 1048576 | tf_op jit(solution)/shard_map/all_to_all | solution.py:450
  19.3 17.1 %copy-start.2 = (bf16[128,2048]{1,0:T(8,128)(2,1)S(1)}, bf16[128,2048]{1,0:T(8,128)(2,1)}, u32[]{:S(2)}) copy-start(bf16[128,2048]{1,0:T(8,128)(2,1)} %param.8) | copy-start | bytes 1572868
  32.4 18.5 %all-to-all-start.1 = ((bf16[128,16,128]{2,0,1:T(8,128)(2,1)}), bf16[128,16,128]{2,0,1:T(8,128)(2,1)S(1)}, u32[]{:S(2)}, u32[]{:S(2)}) async-start(bf16[128,16,128]{2,0,1:T(8,128)(2,1)} %copy.27), calls=%async_computation.1 | async-start | bytes 1048576 | tf_op jit(solution)/shard_map/all_to_all | solution.py:450
  37.7 17.3 %copy-start.3 = (bf16[128,2048]{1,0:T(8,128)(2,1)S(1)}, bf16[128,2048]{1,0:T(8,128)(2,1)}, u32[]{:S(2)}) copy-start(bf16[128,2048]{1,0:T(8,128)(2,1)} %param.10) | copy-start | bytes 1572868
  50.9 18.6 %all-to-all-start.2 = ((bf16[128,16,128]{2,0,1:T(8,128)(2,1)}), bf16[128,16,128]{2,0,1:T(8,128)(2,1)S(1)}, u32[]{:S(2)}, u32[]{:S(2)}) async-start(bf16[128,16,128]{2,0,1:T(8,128)(2,1)} %copy.29), calls=%async_computation.2 | async-start | bytes 1048576 | tf_op jit(solution)/shard_map/all_to_all | solution.py:450
  69.4 0.7 copy-start
  134.6 18.5 %all-to-all-start.5 = ((bf16[16,128,128]{2,1,0:T(8,128)(2,1)}), bf16[16,128,128]{2,1,0:T(8,128)(2,1)S(1)}, u32[]{:S(2)}, u32[]{:S(2)}) async-start(bf16[16,128,128]{2,1,0:T(8,128)(2,1)} %get-tuple-element.10), calls=%async_computation.5 | async-start | bytes 1048576 | tf_op jit(solution)/shard_map/all_to_all | solution.py:454

commit v2 on v1

--- a/solution.py
+++ b/solution.py
@@ -9,6 +9,7 @@
 BLOCK = 64
 CHUNK = 128
 GROUP = 4
+LATE = 2
 F32 = jnp.float32
 BF16 = jnp.bfloat16
 
@@ -171,16 +172,83 @@
 def head_kernel(
     lengths_ref, query_ref, key_ref, value_ref, logit_ref, cotangent_ref,
     query_out, key_out, value_out, logit_out,
+    query_in, key_in, value_in, logit_in, key_back, value_back, logit_back,
     inverse_ref, scores_ref, local_ref, response_ref, offset_ref, step_ref, seed_ref, early_ref,
-    state_ref, adjoint_ref,
+    state_ref, adjoint_ref, in_send, in_recv, out_send, out_recv,
 ):
-    chunks = query_ref.shape[0]
+    chunks = key_in.shape[0]
+    me = lax.axis_index("seq")
     ends = ends_of(lengths_ref)
 
+    def columns(index):
+        return pl.ds(pl.multiple_of(index * CHUNK, CHUNK), CHUNK)
+
+    def ahead(offset):
+        return lax.rem(me + offset, chunks)
+
+    def in_pairs(owner, source):
+        return [
+            (key_ref.at[:, columns(owner)], key_in.at[source]),
+            (value_ref.at[:, columns(owner)], value_in.at[source]),
+            (query_ref.at[:, columns(owner)], query_in.at[source]),
+            (logit_ref.at[owner], logit_in.at[source]),
+        ]
+
+    def out_pairs(index, head):
+        return [
+            (key_back.at[index], key_out.at[:, columns(head)]),
+            (value_back.at[index], value_out.at[:, columns(head)]),
+            (logit_back.at[index], logit_out.at[head]),
+        ]
+
+    def remote(pairs, send, recv, send_at, recv_at, peer):
+        return [
+            pltpu.make_async_remote_copy(
+                src_ref=pair[0],
+                dst_ref=pair[1],
+                send_sem=send.at[i, send_at],
+                recv_sem=recv.at[i, recv_at],
+                device_id={"seq": peer},
+                device_id_type=pl.DeviceIdType.MESH,
+            )
+            for i, pair in enumerate(pairs)
+        ]
+
+    def local_copies(pairs, sems):
+        return [
+            pltpu.make_async_copy(pair[0], pair[1], sems.at[i, me])
+            for i, pair in enumerate(pairs)
+        ]
+
+    barrier = pltpu.get_barrier_semaphore()
+
+    def greet(offset, carry):
+        pl.semaphore_signal(
+            barrier, inc=1, device_id={"seq": ahead(offset)}, device_id_type=pl.DeviceIdType.MESH
+        )
+        return carry
+
+    own = local_copies(in_pairs(me, me), in_recv)
+    for copy in own:
+        copy.start()
+    lax.fori_loop(1, chunks, greet, 0)
+    pl.semaphore_wait(barrier, chunks - 1)
+
+    def send(offset, carry):
+        peer = ahead(offset)
+        for copy in remote(in_pairs(peer, me), in_send, in_recv, peer, me, peer):
+            copy.start()
+        return carry
+
+    lax.fori_loop(1, chunks, send, 0)
+    for copy in own:
+        copy.wait()
+
     def load(index):
-        logit = jnp.broadcast_to(logit_ref[index], (CHUNK, CHUNK))
+        logit = jnp.broadcast_to(logit_in[index], (CHUNK, CHUNK))
         strength = 1.0 / (1.0 + jnp.exp(-logit))
-        return query_ref[index], key_ref[index], value_ref[index], cotangent_ref[index], strength
+        return (query_in[index], key_in[index], value_in[index],
+                cotangent_ref[:, columns(index)], strength)
 
     def store(index, inverse, scores, local, response_k, offset, step, seed, early):
         inverse_ref[index] = inverse
@@ -192,8 +260,20 @@
         seed_ref[index] = seed
         early_ref[index] = early
 
+    def arrive(source):
+        for copy in remote(in_pairs(me, source), in_send, in_recv, source, source, source):
+            copy.wait_recv()
+
     def early_body(turn, carry):
-        prepare([turn * GROUP + i for i in range(GROUP)], ends, load, store)
+        sources = [ahead(chunks - turn * GROUP - i) for i in range(GROUP)]
+
+        @pl.when(turn > 0)
+        def _():
+            arrive(sources[0])
+
+        for source in sources[1:]:
+            arrive(source)
+        prepare(sources, ends, load, store)
         return carry
 
     lax.fori_loop(0, chunks // GROUP, early_body, 0)
@@ -218,33 +298,78 @@
     lax.fori_loop(0, chunks, chain, (zero, zero))
 
     def late_body(turn, carry):
-        for i in range(2):
-            index = turn * 2 + i
+        indices = [ahead(4 + turn * LATE + i) for i in range(LATE)]
+        for index in indices:
             stored = (inverse_ref[index], scores_ref[index], local_ref[index],
                       response_ref[index], early_ref[index])
             results = finish(index, ends, load, stored, state_ref[index], adjoint_ref[index])
-            query_out[index] = results[0]
-            key_out[index] = results[1]
-            value_out[index] = results[2]
-            logit_out[index] = results[3]
+            query_out[:, columns(index)] = results[0]
+            key_back[index] = results[1]
+            value_back[index] = results[2]
+            logit_back[index] = results[3]
+
+        @pl.when(turn != (chunks - 4) // LATE)
+        def _():
+            for copy in remote(
+                out_pairs(indices[0], me), out_send, out_recv, indices[0], me, indices[0]
+            ):
+                copy.start()
+
+        @pl.when(turn == (chunks - 4) // LATE)
+        def _():
+            for copy in local_copies(out_pairs(me, me), out_recv):
+                copy.start()
+
+        for index in indices[1:]:
+            for copy in remote(out_pairs(index, me), out_send, out_recv, index, me, index):
+                copy.start()
         return carry
 
-    lax.fori_loop(0, chunks // 2, late_body, 0)
-
-
-def head_pass(query, key, value, logit, cotangent, lengths, interpret=False):
-    chunks = query.shape[0]
-    square = (chunks, CHUNK, CHUNK)
+    lax.fori_loop(0, chunks // LATE, late_body, 0)
+
+    for copy in local_copies(out_pairs(me, me), out_recv):
+        copy.wait()
+
+    def settle(offset, carry):
+        peer = ahead(offset)
+        for copy in remote(in_pairs(peer, me), in_send, in_recv, peer, me, peer):
+            copy.wait_send()
+        for copy in remote(out_pairs(peer, me), out_send, out_recv, peer, me, peer):
+            copy.wait_send()
+        for copy in remote(out_pairs(me, peer), out_send, out_recv, peer, peer, peer):
+            copy.wait_recv()
+        return carry
+
+    lax.fori_loop(1, chunks, settle, 0)
+
+
+def head_pass(query, key, value, logit, cotangent, lengths):
+    length, width = query.shape
+    heads = logit.shape[0]
+    blocks = (heads, CHUNK, CHUNK)
+    rows = (heads, 1, CHUNK)
     whole = pl.BlockSpec(memory_space=pltpu.VMEM)
+    anywhere = pl.BlockSpec(memory_space=pl.ANY)
     return pl.pallas_call(
         head_kernel,
-        in_specs=[pl.BlockSpec(memory_space=pltpu.SMEM)] + [whole] * 5,
-        out_specs=[whole] * 4,
-        out_shape=[jax.ShapeDtypeStruct(square, BF16)] * 3
-        + [jax.ShapeDtypeStruct((chunks, 1, CHUNK), F32)],
-        scratch_shapes=[pltpu.VMEM(square, F32)] * 10,
-        compiler_params=pltpu.CompilerParams(vmem_limit_bytes=48 << 20),
-        interpret=interpret,
+        in_specs=[pl.BlockSpec(memory_space=pltpu.SMEM), anywhere, anywhere, anywhere, whole, whole],
+        out_specs=[whole, anywhere, anywhere, whole],
+        out_shape=[
+            jax.ShapeDtypeStruct((CHUNK, width), BF16),
+            jax.ShapeDtypeStruct((length, width), BF16),
+            jax.ShapeDtypeStruct((length, width), BF16),
+            jax.ShapeDtypeStruct(rows, F32),
+        ],
+        scratch_shapes=[pltpu.VMEM(blocks, BF16)] * 3
+        + [pltpu.VMEM(rows, F32)]
+        + [pltpu.VMEM(blocks, BF16)] * 2
+        + [pltpu.VMEM(rows, F32)]
+        + [pltpu.VMEM(blocks, F32)] * 10
+        + [pltpu.SemaphoreType.DMA((4, heads))] * 2
+        + [pltpu.SemaphoreType.DMA((3, heads))] * 2,
+        compiler_params=pltpu.CompilerParams(
+            vmem_limit_bytes=48 << 20, collective_id=0, has_side_effects=True
+        ),
     )(lengths, query, key, value, logit, cotangent)
 
 
@@ -438,38 +563,16 @@
     devices = lax.axis_size("seq")
     length, width = query_acts.shape
     head_count = beta_logit.shape[0]
-    window = length * devices
-    chunks = window // CHUNK
-    by_heads = devices == head_count and width == head_count * CHUNK and chunks % GROUP == 0
-    if not by_heads or window % CHUNK:
+    by_heads = devices == head_count and width == head_count * CHUNK and length == CHUNK
+    if not by_heads or devices % GROUP or devices < 8:
         return shards_by_tokens(
             query_acts, key_acts, value_acts, beta_logit, output_grad, doc_lengths
         )
-
-    def to_heads(values):
-        moved = lax.all_to_all(values, "seq", split_axis=1, concat_axis=0, tiled=True)
-        return moved.reshape(chunks, CHUNK, CHUNK)
-
-    def to_tokens(values):
-        return lax.all_to_all(
-            values.reshape(window, CHUNK), "seq", split_axis=0, concat_axis=1, tiled=True
-        )
-
-    logit = lax.all_to_all(beta_logit, "seq", split_axis=0, concat_axis=1, tiled=True)
-    cotangent = output_grad.reshape(CHUNK, chunks, CHUNK).transpose(1, 0, 2)
-    grads = head_pass(
-        to_heads(query_acts),
-        to_heads(key_acts),
-        to_heads(value_acts),
-        logit.reshape(chunks, 1, CHUNK),
-        cotangent,
-        doc_lengths,
-    )
-    query_grad = grads[0].transpose(1, 0, 2).reshape(CHUNK, window)
-    logit_grad = lax.all_to_all(
-        grads[3].reshape(1, window), "seq", split_axis=1, concat_axis=0, tiled=True
-    )
-    return query_grad, to_tokens(grads[1]), to_tokens(grads[2]), logit_grad
+    logit = beta_logit.reshape(head_count, 1, length)
+    query_grad, key_grad, value_grad, logit_grad = head_pass(
+        query_acts, key_acts, value_acts, logit, output_grad, doc_lengths
+    )
+    return query_grad, key_grad, value_grad, logit_grad.reshape(head_count, length)
 
 
 def solution(mesh):

time: 156 us -> 89.1 us (0.57)
  waiting for transfers between devices: 56 us -> 0 us
  Pallas kernels: 37.1 us -> 79.5 us
  blocking collectives: 27.4 us -> 0 us
  starting transfers between devices: 23.1 us -> 0 us
  local copies, waits for them, and re-layouts: 10.7 us -> 8.49 us
    all_to_all x5 -> x0, waiting for transfers between devices: 56 us -> none  [the longest x3 40.1 us: to_heads(): lax.all_to_all(values, 'seq', split_axis=1, concat_axis=0, tiled=True)]
    pallas_call x1, Pallas kernels: 37.1 us -> 79.5 us  [head_pass(): pl.pallas_call(head_kernel, in_specs=[pl.BlockSpec(memory_space=pltpu.SME...]
    all_to_all x2 -> x0, blocking collectives: 27.4 us -> none  [the longest x1 17.1 us: to_tokens(): lax.all_to_all(values.reshape(window, CHUNK), 'seq', split_axis=0, concat...]
    all_to_all x5 -> x0, starting transfers between devices: 23.1 us -> none  [the longest x3 11.7 us: to_heads(): lax.all_to_all(values, 'seq', split_axis=1, concat_axis=0, tiled=True)]
    all_to_all x5 -> x0, local copies, waits for them, and re-layouts: 3.64 us -> none  [the longest x3 3.06 us: to_heads(): lax.all_to_all(values, 'seq', split_axis=1, concat_axis=0, tiled=True)]
    unnamed x16, local copies, waits for them, and re-layouts: 6.45 us -> 8.49 us
  transfers between devices with their start and end apart: 5 -> 0, of which waited for: 5 -> 0; matrix products, arithmetic and copies ran while one was open for 5% -> 0% of each run, Pallas kernels for 0% -> 0%
where the time goes in v2:
time: 89.1 us; the launch traced here: 88.6 us
  Pallas kernels  79.5 us (89%)
  local copies, waits for them, and re-layouts  8.49 us (10%)
    pallas_call x1, Pallas kernels, head_pass(): pl.pallas_call(head_kernel, in_specs=[pl.BlockSpec(memory_space=pltpu.SME...  79.5 us
    unnamed x16, local copies, waits for them, and re-layouts  8.49 us

profile of v2, /device:TPU:0, one launch (start us, length us, event | category | flops | bytes accessed | tf_op | source)
XLA Modules:
  0.0 88.6 jit_solution(4074255026603806794)
XLA Ops:
  0.6 0.0 copy-start.5
  0.6 0.6 copy-done.5
  1.3 0.0 copy-start
  1.3 1.0 %copy-done = bf16[128,2048]{1,0:T(8,128)(2,1)S(1)} copy-done((bf16[128,2048]{1,0:T(8,128)(2,1)S(1)}, bf16[128,2048]{1,0:T(8,128)(2,1)}, u32[]{:S(2)}) %copy-start) | copy-done | bytes 524312
  2.3 0.0 copy-start.1
  2.3 1.0 %copy-done.1 = bf16[128,2048]{1,0:T(8,128)(2,1)S(1)} copy-done((bf16[128,2048]{1,0:T(8,128)(2,1)S(1)}, bf16[128,2048]{1,0:T(8,128)(2,1)}, u32[]{:S(2)}) %copy-start.1) | copy-done | bytes 524312
  3.4 0.0 copy-start.2
  3.4 1.0 %copy-done.2 = bf16[128,2048]{1,0:T(8,128)(2,1)S(1)} copy-done((bf16[128,2048]{1,0:T(8,128)(2,1)S(1)}, bf16[128,2048]{1,0:T(8,128)(2,1)}, u32[]{:S(2)}) %copy-start.2) | copy-done | bytes 524312
  4.4 0.0 copy-start.3
  4.4 1.0 %copy-done.3 = bf16[128,2048]{1,0:T(8,128)(2,1)S(1)} copy-done((bf16[128,2048]{1,0:T(8,128)(2,1)S(1)}, bf16[128,2048]{1,0:T(8,128)(2,1)}, u32[]{:S(2)}) %copy-start.3) | copy-done | bytes 524312
  5.5 0.0 copy-start.4
  5.5 0.7 copy-done.4
  6.2 79.5 %shard_map.93 = (bf16[128,2048]{1,0:T(8,128)(2,1)S(1)}, bf16[128,2048]{1,0:T(8,128)(2,1)S(1)}, bf16[128,2048]{1,0:T(8,128)(2,1)S(1)}, f32[16,1,128]{2,1,0:T(1,128)S(1)}) custom-call(s32[4]{0:T(128)S(1)} %copy-done.5, bf16[128,2048]{1,0:T(8,128)(2,1)S(1)} %copy-done, bf16[128,2048]{1,0:T(8,128)(2,1)S(1)} %copy-done.1, bf16[128,2048]{1,0:T(8,128)(2,1)S(1)} %copy-done.2, ...), custom_call_target="tpu_custom_call" | custom-call | tf_op jit(solution)/shard_map/pallas_call | solution.py:353
  85.6 0.8 copy.14
  86.4 0.8 copy.15
  87.2 0.8 copy.16
  88.0 0.6 copy.17
Async XLA Ops:
  0.6 0.7 copy-start.5
  1.3 1.0 %copy-start = (bf16[128,2048]{1,0:T(8,128)(2,1)S(1)}, bf16[128,2048]{1,0:T(8,128)(2,1)}, u32[]{:S(2)}) copy-start(bf16[128,2048]{1,0:T(8,128)(2,1)} %query_ref.1) | copy-start | bytes 1572868
  2.3 1.0 %copy-start.1 = (bf16[128,2048]{1,0:T(8,128)(2,1)S(1)}, bf16[128,2048]{1,0:T(8,128)(2,1)}, u32[]{:S(2)}) copy-start(bf16[128,2048]{1,0:T(8,128)(2,1)} %key_ref.1) | copy-start | bytes 1572868
  3.4 1.0 %copy-start.2 = (bf16[128,2048]{1,0:T(8,128)(2,1)S(1)}, bf16[128,2048]{1,0:T(8,128)(2,1)}, u32[]{:S(2)}) copy-start(bf16[128,2048]{1,0:T(8,128)(2,1)} %value_ref.1) | copy-start | bytes 1572868
  4.4 1.0 %copy-start.3 = (bf16[128,2048]{1,0:T(8,128)(2,1)S(1)}, bf16[128,2048]{1,0:T(8,128)(2,1)}, u32[]{:S(2)}) copy-start(bf16[128,2048]{1,0:T(8,128)(2,1)} %cotangent_ref.1) | copy-start | bytes 1572868
  5.5 0.7 copy-start.4

commit v3 on v2

--- a/solution.py
+++ b/solution.py
@@ -174,7 +174,7 @@
     query_out, key_out, value_out, logit_out,
     query_in, key_in, value_in, logit_in, key_back, value_back, logit_back,
     inverse_ref, scores_ref, local_ref, response_ref, offset_ref, step_ref, seed_ref, early_ref,
-    state_ref, adjoint_ref, in_send, in_recv, out_send, out_recv,
+    state_ref, adjoint_ref, turned_ref, turned_sem, in_send, in_recv, out_send, out_recv,
 ):
     chunks = key_in.shape[0]
     me = lax.axis_index("seq")
@@ -231,6 +231,8 @@
     own = local_copies(in_pairs(me, me), in_recv)
     for copy in own:
         copy.start()
+    turned = pltpu.make_async_copy(cotangent_ref, turned_ref, turned_sem)
+    turned.start()
     lax.fori_loop(1, chunks, greet, 0)
     pl.semaphore_wait(barrier, chunks - 1)
 
@@ -243,12 +245,13 @@
     lax.fori_loop(1, chunks, send, 0)
     for copy in own:
         copy.wait()
+    turned.wait()
 
     def load(index):
         logit = jnp.broadcast_to(logit_in[index], (CHUNK, CHUNK))
         strength = 1.0 / (1.0 + jnp.exp(-logit))
         return (query_in[index], key_in[index], value_in[index],
-                cotangent_ref[:, columns(index)], strength)
+                turned_ref[:, columns(index)], strength)
 
     def store(index, inverse, scores, local, response_k, offset, step, seed, early):
         inverse_ref[index] = inverse
@@ -352,7 +355,7 @@
     anywhere = pl.BlockSpec(memory_space=pl.ANY)
     return pl.pallas_call(
         head_kernel,
-        in_specs=[pl.BlockSpec(memory_space=pltpu.SMEM), anywhere, anywhere, anywhere, whole, whole],
+        in_specs=[pl.BlockSpec(memory_space=pltpu.SMEM), anywhere, anywhere, anywhere, anywhere, anywhere],
         out_specs=[whole, anywhere, anywhere, whole],
         out_shape=[
             jax.ShapeDtypeStruct((CHUNK, width), BF16),
@@ -365,10 +368,11 @@
         + [pltpu.VMEM(blocks, BF16)] * 2
         + [pltpu.VMEM(rows, F32)]
         + [pltpu.VMEM(blocks, F32)] * 10
+        + [pltpu.VMEM((CHUNK, width), BF16), pltpu.SemaphoreType.DMA]
         + [pltpu.SemaphoreType.DMA((4, heads))] * 2
         + [pltpu.SemaphoreType.DMA((3, heads))] * 2,
         compiler_params=pltpu.CompilerParams(
-            vmem_limit_bytes=48 << 20, collective_id=0, has_side_effects=True
+            vmem_limit_bytes=63 << 20, collective_id=0, has_side_effects=True
         ),
     )(lengths, query, key, value, logit, cotangent)
 

time: 89.1 us -> 86.2 us (0.967)
  local copies, waits for them, and re-layouts: 8.49 us -> 4.57 us
  Pallas kernels: 79.5 us -> 80.7 us
    unnamed x16 -> x10, local copies, waits for them, and re-layouts: 8.49 us -> 4.57 us
    pallas_call x1, Pallas kernels: 79.5 us -> 80.7 us  [head_pass(): pl.pallas_call(head_kernel, in_specs=[pl.BlockSpec(memory_space=pltpu.SME...]
where the time goes in v3:
time: 86.2 us; the launch traced here: 85.9 us
  Pallas kernels  80.7 us (94%)
  local copies, waits for them, and re-layouts  4.57 us (5%)
    pallas_call x1, Pallas kernels, head_pass(): pl.pallas_call(head_kernel, in_specs=[pl.BlockSpec(memory_space=pltpu.SME...  80.7 us
    unnamed x10, local copies, waits for them, and re-layouts  4.57 us

profile of v3, /device:TPU:0, one launch (start us, length us, event | category | flops | bytes accessed | tf_op | source)
XLA Modules:
  0.0 85.9 jit_solution(16849722276309797542)
XLA Ops:
  0.6 80.7 %shard_map.93 = (bf16[128,2048]{1,0:T(8,128)(2,1)}, bf16[128,2048]{1,0:T(8,128)(2,1)}, bf16[128,2048]{1,0:T(8,128)(2,1)}, f32[16,1,128]{2,1,0:T(1,128)}) custom-call(s32[4]{0:T(128)} %lengths_ref.1, bf16[128,2048]{1,0:T(8,128)(2,1)} %query_ref.1, bf16[128,2048]{1,0:T(8,128)(2,1)} %key_ref.1, bf16[128,2048]{1,0:T(8,128)(2,1)} %value_ref.1, ...), custom_call_target="tpu_custom_call" | custom-call | tf_op jit(solution)/shard_map/pallas_call | solution.py:356
  81.3 0.0 copy-start.1
  81.3 1.9 %copy.14 = bf16[128,2048]{1,0:T(8,128)(2,1)} copy(bf16[128,2048]{1,0:T(8,128)(2,1)} %get-tuple-element.16) | data formatting | bytes 1048576
  83.3 0.0 copy-done.1
  83.3 0.0 copy-start
  83.3 0.8 copy.15
  84.1 0.4 copy-done
  84.5 0.0 copy-start.2
  84.5 0.8 copy.16
  85.3 0.0 copy-done.2
  85.3 0.6 copy.17
Async XLA Ops:
  81.3 2.0 %copy-start.1 = (bf16[128,2048]{1,0:T(8,128)(2,1)S(1)}, bf16[128,2048]{1,0:T(8,128)(2,1)}, u32[]{:S(2)}) copy-start(bf16[128,2048]{1,0:T(8,128)(2,1)} %get-tuple-element.17) | copy-start | bytes 1572868
  83.3 1.2 %copy-start = (bf16[128,2048]{1,0:T(8,128)(2,1)S(1)}, bf16[128,2048]{1,0:T(8,128)(2,1)}, u32[]{:S(2)}) copy-start(bf16[128,2048]{1,0:T(8,128)(2,1)} %get-tuple-element.18) | copy-start | bytes 1572868
  84.5 0.8 copy-start.2
